TPU v7x, 32 devices: a whole 2x2x4 slice. The times are simulated.
32 devices in a mesh: groups: 1, row: 16 (over z, y, core), col: 2 (over x).
Axes of the slice: x: 2, y: 2, z: 4, core: 2. Of those that a mesh axis runs over, the one named last changes fastest.
Arguments:
- pair_grid: bfloat16 [256, 256, 128], P(('groups', 'row'), 'col'), may hold values from -6 to 6
- alignment_pool: bfloat16 [256, 256, 64], P('groups', 'row'), may hold values from -6 to 6
- sample_index: int32 [64], P('groups'), may hold values from 0 to 255
- token_mask: int32 [256], P('groups'), may hold values 0 or 1
- outer_proj: bfloat16 [64, 64], replicated, may hold values from -0.75 to 0.75
- outer_mix: bfloat16 [1024, 128], replicated, may hold values from -0.375 to 0.375
- pair_logit: bfloat16 [128, 8], replicated, may hold values from -1 to 1
- average_proj: bfloat16 [64, 512], replicated, may hold values from -0.75 to 0.75
- average_mix: bfloat16 [256, 64], replicated, may hold values from -0.75 to 0.75
- triangle_proj: bfloat16 [128, 640], replicated, may hold values from -0.5 to 0.5
- triangle_mix: bfloat16 [128, 128], replicated, may hold values from -0.5 to 0.5
- transition_up: bfloat16 [128, 1024], replicated, may hold values from -0.5 to 0.5
- transition_down: bfloat16 [512, 128], replicated, may hold values from -0.25 to 0.25
Outputs:
- pair_next: bfloat16 [256, 256, 128], P(('groups', 'row'), 'col')
- alignment_next: bfloat16 [64, 256, 64], P('groups', 'row')
Inputs may be any that keep to these rules, and one draw needn't show every extreme that they name: `sample_index`: indices into the first dimension of alignment_pool; they may repeat. `token_mask`: 1 marks a real residue, 0 a padded one.
All inputs are finite; a program needn't handle non-finite values.
Results may differ from a plain program's by a relative error of at most 0.008.
Values may be sent and summed in bfloat16 or wider, within the bound.
A program may use at most 64 MiB of HBM per device.

v0:
```python
import jax
import jax.numpy as jnp
from jax import lax
from jax.sharding import PartitionSpec as P

epsilon = 1e-05


def normalize(values, channel_dim):
    values = values.astype(jnp.float32)
    centred = values - jnp.mean(values, axis=channel_dim, keepdims=True)
    spread = jnp.mean(centred * centred, axis=channel_dim, keepdims=True)
    return centred / jnp.sqrt(spread + epsilon)


def triangle_product(exchanged, n_row, n_col):
    left_part = exchanged[0]
    right_part = exchanged[1]
    item_count = left_part.shape[2]
    tok_row = left_part.shape[3]
    tok_col = left_part.shape[4]
    product = jnp.einsum(
        "ruxiq,suxjq->xrisj", left_part, right_part, preferred_element_type=jnp.float32
    )
    product = product.reshape(item_count, n_row, tok_row, n_col, tok_col)
    return product.transpose(1, 3, 0, 2, 4).astype(jnp.bfloat16)


def on_device(
    pair_grid,
    alignment_pool,
    sample_index,
    token_mask,
    outer_proj,
    outer_mix,
    pair_logit,
    average_proj,
    average_mix,
    triangle_proj,
    triangle_mix,
    transition_up,
    transition_down,
):
    n_row = lax.axis_size("row")
    n_col = lax.axis_size("col")
    tok_row = pair_grid.shape[0]
    tok_col = pair_grid.shape[1]
    pair_width = pair_grid.shape[2]
    samples = sample_index.shape[0]
    align_width = alignment_pool.shape[2]
    outer_width = outer_proj.shape[1] // 2
    head_count = pair_logit.shape[1]
    head_total = average_proj.shape[1] // 2
    head_dim = head_total // head_count
    inner_width = transition_down.shape[0]
    row_start = lax.axis_index("row") * tok_row
    column_start = lax.axis_index("col") * tok_col
    alignments = jnp.take(alignment_pool, sample_index, axis=0)
    align_norm = normalize(alignments, 2).astype(jnp.bfloat16)
    align_rows = align_norm.reshape(samples, tok_row * align_width)
    gathered = lax.all_gather(align_rows, "row", axis=1, tiled=True)
    column_flat = lax.dynamic_slice_in_dim(
        gathered, column_start * align_width, tok_col * align_width, 1
    )
    column_norm = column_flat.reshape(samples, tok_col, align_width)
    row_factor = jnp.dot(
        align_norm, outer_proj[:, :outer_width], preferred_element_type=jnp.float32
    ).astype(jnp.bfloat16)
    column_factor = jnp.dot(
        column_norm, outer_proj[:, outer_width:], preferred_element_type=jnp.float32
    ).astype(jnp.bfloat16)
    column_rows = column_factor.reshape(samples, tok_col * outer_width)
    block_rows = 8
    block_count = tok_row // block_rows
    row_blocks = row_factor.reshape(samples, block_count, block_rows * outer_width).transpose(
        1, 0, 2
    )
    pair_blocks = pair_grid.reshape(block_count, block_rows, tok_col, pair_width)

    def outer_step(operands):
        left_block, pair_block = operands
        outer_sum = lax.dot_general(
            left_block, column_rows, (((0,), (0,)), ((), ())), preferred_element_type=jnp.float32
        )
        outer_sum = outer_sum.reshape(block_rows, outer_width, tok_col, outer_width).transpose(
            0, 2, 1, 3
        )
        outer_mean = (
            (outer_sum * (1.0 / samples))
            .astype(jnp.bfloat16)
            .reshape(block_rows * tok_col, outer_width * outer_width)
        )
        update = jnp.dot(outer_mean, outer_mix, preferred_element_type=jnp.float32).reshape(
            block_rows, tok_col, pair_width
        )
        return (pair_block.astype(jnp.float32) + update).astype(jnp.bfloat16)

    pair_one = lax.map(outer_step, (row_blocks, pair_blocks)).reshape(tok_row, tok_col, pair_width)
    pair_norm = normalize(pair_one, 2).astype(jnp.bfloat16)
    value_weight = average_proj[:, :head_total].reshape(align_width, head_count, head_dim)
    gate_weight = average_proj[:, head_total:].reshape(align_width, head_count, head_dim)
    mix_weight = average_mix.reshape(head_count, head_dim, align_width)
    scores = lax.dot_general(
        pair_logit, pair_norm, (((0,), (2,)), ((), ())), preferred_element_type=jnp.float32
    )
    weights = jnp.exp(scores)
    partial_total = jnp.sum(weights, axis=2)
    weights_low = weights.astype(jnp.bfloat16)
    column_values = jnp.einsum(
        "sjm,mhc->hjsc", column_norm, value_weight, preferred_element_type=jnp.float32
    )
    column_values = column_values.astype(jnp.bfloat16).reshape(
        head_count, tok_col, samples * head_dim
    )
    partial_sum = jnp.einsum(
        "hij,hjk->hik", weights_low, column_values, preferred_element_type=jnp.float32
    )
    weighted, totals = (
        lax.psum(partial_sum.astype(jnp.bfloat16), "col").astype(jnp.float32),
        lax.psum(partial_total.astype(jnp.bfloat16), "col").astype(jnp.float32),
    )
    gate_values = jax.nn.sigmoid(
        jnp.einsum("sim,mhc->hisc", align_norm, gate_weight, preferred_element_type=jnp.float32)
    )
    weighted = weighted.reshape(head_count, tok_row, samples, head_dim)
    averaged = (gate_values * weighted / totals[:, :, None, None]).astype(jnp.bfloat16)
    align_update = jnp.einsum(
        "hisc,hcm->sim", averaged, mix_weight, preferred_element_type=jnp.float32
    )
    alignment_next = (alignments.astype(jnp.float32) + align_update).astype(jnp.bfloat16)
    flat_norm = pair_norm.reshape(tok_row * tok_col, pair_width)
    projected = lax.dot_general(
        triangle_proj[:, : 4 * pair_width],
        flat_norm,
        (((0,), (1,)), ((), ())),
        preferred_element_type=jnp.float32,
    )
    projected = projected.reshape(4, pair_width, tok_row, tok_col)
    row_mask = lax.dynamic_slice_in_dim(token_mask, row_start, tok_row, 0).astype(jnp.float32)
    column_mask = lax.dynamic_slice_in_dim(token_mask, column_start, tok_col, 0).astype(jnp.float32)
    pair_mask = row_mask[:, None] * column_mask[None, :]
    left_side = jax.nn.sigmoid(projected[0]) * projected[1] * pair_mask
    right_side = jax.nn.sigmoid(projected[2]) * projected[3] * pair_mask
    factors = jnp.stack([left_side, right_side]).astype(jnp.bfloat16)
    group_size = pair_width // (n_row * n_col)
    grouped = factors.reshape(2, n_row * n_col, group_size, tok_row, tok_col)
    received = lax.all_to_all(grouped, ("row", "col"), split_axis=1, concat_axis=1, tiled=True)
    arranged = received.reshape(2, n_row, n_col, received.shape[2], tok_row, tok_col)
    result = triangle_product(arranged, n_row, n_col)
    flat_result = result.reshape(n_row * n_col, result.shape[2], tok_row, tok_col)
    product = lax.all_to_all(flat_result, ("row", "col"), split_axis=0, concat_axis=0, tiled=True)
    product = product.reshape(pair_width, tok_row, tok_col)
    product_norm = normalize(product, 0).astype(jnp.bfloat16).reshape(pair_width, tok_row * tok_col)
    mixed = lax.dot_general(
        product_norm, triangle_mix, (((0,), (0,)), ((), ())), preferred_element_type=jnp.float32
    )
    gate_out = jax.nn.sigmoid(
        jnp.dot(flat_norm, triangle_proj[:, 4 * pair_width :], preferred_element_type=jnp.float32)
    )
    pair_two = (
        pair_one.reshape(tok_row * tok_col, pair_width).astype(jnp.float32) + gate_out * mixed
    ).astype(jnp.bfloat16)
    tail_rows = pair_two.reshape(block_count, block_rows * tok_col, pair_width)

    def transition_step(rows_block):
        normed = normalize(rows_block, 1).astype(jnp.bfloat16)
        expanded = jnp.dot(normed, transition_up, preferred_element_type=jnp.float32)
        hidden = (jax.nn.silu(expanded[:, :inner_width]) * expanded[:, inner_width:]).astype(
            jnp.bfloat16
        )
        return (
            rows_block.astype(jnp.float32)
            + jnp.dot(hidden, transition_down, preferred_element_type=jnp.float32)
        ).astype(jnp.bfloat16)

    pair_next = lax.map(transition_step, tail_rows).reshape(tok_row, tok_col, pair_width)
    return (pair_next, alignment_next)


def solution(mesh):
    in_specs = (
        P(("groups", "row"), "col", None),
        P("groups", "row", None),
        P("groups"),
        P("groups"),
        P(),
        P(),
        P(),
        P(),
        P(),
        P(),
        P(),
        P(),
        P(),
    )
    out_specs = (P(("groups", "row"), "col", None), P("groups", "row", None))
    return jax.shard_map(
        on_device, mesh=mesh, in_specs=in_specs, out_specs=out_specs, check_vma=False
    )
```

profile of v0, /device:TPU:0, one launch (start us, length us, event | category | flops | bytes accessed | tf_op | source)
XLA Modules:
  0.0 163.6 jit_solution(2614358065298384016)
XLA Ops:
  7.2 0.7 compare_select_fusion
  7.9 0.7 compare_and_fusion
  8.5 2.0 %copy.82 = bf16[256,16,64]{2,1,0:T(8,128)(2,1)S(1)} copy(bf16[256,16,64]{0,2,1:T(8,128)(2,1)} %param.18) | data formatting | bytes 1048576 | tf_op args[1]
  10.6 0.6 gather_fusion
  11.2 0.3 convert_reduce_fusion.2
  11.5 0.4 fusion.52
  13.1 0.8 divide_convert_fusion
  14.1 1.2 convolution_convert_fusion.2
  15.3 42.9 %all-gather.2.cloned.1.call-done = bf16[64,16384]{1,0:T(8,128)(2,1)} async-done(((bf16[64,1024]{1,0:T(8,128)(2,1)}), bf16[64,16384]{1,0:T(8,128)(2,1)}) %all-gather.2.cloned.1.call-update) | async-done | bytes 2097168 | tf_op jit(solution)/shard_map/all_gather | solution.py:61
  58.2 2.3 %constant_dynamic-slice_fusion.1 = bf16[64,8192]{1,0:T(8,128)(2,1)} fusion(bf16[64,16384]{1,0:T(8,128)(2,1)} %all-gather.2.cloned.1.call-done, s32[]{:T(128)S(6)} %select_n.24), kind=kLoop, calls=%fused_computation.116 | loop fusion | bytes 2097156 | tf_op jit(solution)/shard_map/dynamic_slice | solution.py:62
  60.5 3.3 %reshape.294 = bf16[64,128,64]{2,1,0:T(8,128)(2,1)S(1)} reshape(bf16[64,8192]{1,0:T(8,128)(2,1)} %constant_dynamic-slice_fusion.1) | data formatting | bytes 2097152 | tf_op jit(solution)/shard_map/reshape | solution.py:65
  63.8 1.3 copy-done.1
  65.1 0.9 convolution_convert_fusion.1
  66.0 1.7 %copy.89 = bf16[64,128,32]{0,2,1:T(8,128)(2,1)S(1)} copy(bf16[64,128,32]{1,2,0:T(8,128)(2,1)S(1)} %convolution_convert_fusion.1) | data formatting | bytes 1048576 | tf_op jit(solution)/shard_map/convert_element_type | solution.py:71
  67.7 9.3 %while.20 = (s32[]{:T(128)}, bf16[2,8,128,128]{3,2,1,0:T(8,128)(2,1)S(1)}, bf16[2,8,128,128]{3,2,1,0:T(8,128)(2,1)}, bf16[2,64,256]{1,2,0:T(8,128)(2,1)}, bf16[6...) while((s32[]{:T(128)}, bf16[2,8,128,128]{3,2,1,0:T(8,128)(2,1)S(1)}, ...), condition=%wide.region_3.4_spmd, body=%wide.region_2.3_spmd.sunk | while | flops 405143552 | bytes 13992077 | solution.py:98
  67.7 0.8 constant_dynamic-slice_fusion.3
  68.6 1.1 copy.148
  69.7 0.7 fusion.111
  70.4 0.8 copy.149
  71.5 0.9 fusion.112
  72.4 0.8 constant_dynamic-slice_fusion.3
  73.2 1.1 copy.148
  74.3 0.7 fusion.111
  75.0 0.8 copy.149
  76.1 0.9 fusion.112
  77.2 0.6 fusion.47
  77.9 0.6 fusion.45
  78.5 0.8 copy-done.4
  79.3 0.7 convolution_bitcast_fusion
  80.0 1.6 slice_multiply_fusion.2
  81.5 0.3 copy.90
  82.1 1.6 copy.91
  83.8 0.3 multiply_convert_fusion.2
  84.2 1.2 copy.92
  85.5 3.5 %all-to-all-start = ((bf16[2,32,4,16,128]{4,3,2,0,1:T(8,128)(2,1)}), bf16[2,32,4,16,128]{4,3,2,0,1:T(8,128)(2,1)}, u32[]{:S(2)}, u32[]{:S(2)}) async-start(bf16[2,32,4,16,128]{4,3,2,0,1:T(8,128)(2,1)} %copy.92), calls=%async_computation | async-start | bytes 2097152 | tf_op jit(solution)/shard_map/all_to_all | solution.py:147
  88.9 0.3 all-reduce.2.cloned.1.call-start
  89.4 1.3 convert_bitcast_fusion.1
  90.6 0.9 copy.100
  91.5 0.6 fusion.43
  92.1 0.3 fusion.77
  92.5 1.2 convolution_convert_fusion
  93.7 1.6 %reshape.302 = bf16[8,16,64,32]{3,2,1,0:T(8,128)(2,1)S(1)} reshape(bf16[8,16,2048]{2,1,0:T(8,128)(2,1)S(1)} %convolution_convert_fusion) | data formatting | bytes 1048576 | tf_op jit(solution)/shard_map/reshape | solution.py:125
  95.3 1.6 copy.103
  97.0 18.1 %all-to-all-done = bf16[2,32,4,16,128]{4,3,2,0,1:T(8,128)(2,1)} async-done(((bf16[2,32,4,16,128]{4,3,2,0,1:T(8,128)(2,1)}), bf16[2,32,4,16,128]{4,3,2,0,1:T(8,128)(2,1)}, u32[]{:S(2)}, u32[]{:S(2)}) %all-to-all-start) | async-done | bytes 1048608 | tf_op jit(solution)/shard_map/all_to_all | solution.py:147
  115.1 1.4 fusion.76
  116.6 1.3 bitcast_convert_fusion
  117.9 3.0 %copy.95 = bf16[4,16,16,16,16]{4,3,2,1,0:T(8,128)(2,1)} copy(bf16[4,16,16,16,16]{4,2,3,1,0:T(8,128)(2,1)S(1)} %bitcast_convert_fusion) | data formatting | bytes 1048576 | tf_op jit(solution)/shard_map/convert_element_type | solution.py:26
  120.9 5.8 %convert_element_type.146 = bf16[4,16,16,2,128]{4,3,2,1,0:T(2,128)(2,1)S(1)} reshape(bf16[4,16,16,16,16]{4,3,2,1,0:T(8,128)(2,1)} %copy.95) | data formatting | bytes 1048576 | tf_op jit(solution)/shard_map/convert_element_type | solution.py:26
  126.7 0.9 copy.96
  127.7 3.6 %all-to-all-start.1 = ((bf16[32,4,16,128]{3,2,1,0:T(8,128)(2,1)}), bf16[32,4,16,128]{3,2,1,0:T(8,128)(2,1)S(1)}, u32[]{:S(2)}, u32[]{:S(2)}) async-start(bf16[32,4,16,128]{3,2,1,0:T(8,128)(2,1)} %bitcast.34), calls=%async_computation.1 | async-start | bytes 1048576 | tf_op jit(solution)/shard_map/all_to_all | solution.py:151
  131.6 8.5 %psum.15 = bf16[8,16]{1,0:T(8,128)(2,1)S(1)} all-reduce(bf16[8,16]{1,0:T(8,128)(2,1)S(1)} %copy.104), channel_id=1, replica_groups=mesh['groups'=1,'row'=16,'col'=2] {'col'}, use_global_device_ids=true, to_apply=%region_14.15 | all-reduce | flops 128 | bytes 512 | tf_op jit(solution)/shard_map/psum | solution.py:120
  140.2 2.1 %fusion.26 = f32[2048,128]{1,0:T(8,128)} fusion(bf16[2048,128]{1,0:T(8,128)(2,1)S(1)} %copy-done.5, bf16[128,640]{1,0:T(8,128)(2,1)} %param.26), kind=kOutput, calls=%fused_computation.39 | convolution fusion | flops 67895296 | bytes 1605632 | tf_op jit(solution)/shard_map/dot_general | solution.py:158
  142.3 3.7 %all-reduce.2.cloned.1.call-done = bf16[8,16,64,32]{2,3,1,0:T(8,128)(2,1)} async-done(((bf16[8,16,64,32]{2,3,1,0:T(8,128)(2,1)}), bf16[8,16,64,32]{2,3,1,0:T(8,128)(2,1)}) %all-reduce.2.cloned.1.call-update) | async-done | bytes 524304 | tf_op jit(solution)/shard_map/psum | solution.py:119
  146.1 2.5 %fusion.32 = bf16[64,16,64]{2,0,1:T(8,128)(2,1)S(1)} fusion(bf16[8,32,64,1]{2,1,3,0:T(8,128)(2,1)S(1)} %bitcast.239, bf16[8,16,64,32]{2,3,1,0:T(8,128)(2,1)} %all-reduce.2.cloned.1.call-done, bf16[64,8,32,1]{0,2,3,1:T(8,128)(2,1)S(1)} %bitcast.238, f32[8,16]{1,0:T(8,128)S(1)} %convert_element_type.161, f32[64,16]{0,1:T(8,128)S(1)} %add_sqrt_fusion.2, ...), kind=kOutput, calls=%fused_computation.49 | convolution fusion | flops 69533696 | bytes 860736 | tf_op jit(solution)/shard_map/hisc,hcm->sim/dot_general | solution.py:127
  148.5 0.9 copy.106
  149.9 1.8 %fusion.27 = bf16[2048,128]{1,0:T(8,128)(2,1)S(1)} fusion(f32[2048,128]{1,0:T(8,128)} %fusion.26, bf16[128,128]{1,0:T(8,128)(2,1)S(1)} %copy-done, f32[16,8,16,128]{3,2,1,0:T(8,128)S(1)} %bitcast_convert_fusion.1, f32[2048]{0:T(1024)S(1)} %sqrt_bitcast_fusion, f32[2048]{0:T(1024)S(1)} %get-tuple-element.106, bf16[2048,128]{1,0:T(8,128)(2,1)S(1)} %bitcast.227), kind=kOutput, calls=%fused_computation.41 | convolution fusion | flops 68943872 | bytes 3194880 | tf_op jit(solution)/shard_map/dot_general | solution.py:154
  151.8 4.2 %while.21 = (s32[]{:T(128)}, bf16[2,1024,128]{2,1,0:T(8,128)(2,1)S(1)}, bf16[2,1024,128]{2,1,0:T(8,128)(2,1)S(1)}, bf16[128,1024]{1,0:T(8,128)(2,1)S(1)}, bf16[512,128]{1,0:T(8,128)(2,1)S(1)}, /*index=5*/s32[]{:T(128)}) while((s32[]{:T(128)}, bf16[2,1024,128]{2,1,0:T(8,128)(2,1)S(1)}, bf16[2,1024,128]{2,1,0:T(8,128)(2,1)S(1)}, ...), condition=%wide.region_11.12_spmd, body=%wide.region_8.11_spmd.sunk | while | flops 407503872 | bytes 10129493 | solution.py:176
  151.9 0.4 fusion.117
  152.3 0.8 fusion.118
  153.1 0.8 fusion.119
  154.1 0.4 fusion.117
  154.4 0.8 fusion.118
  155.2 0.8 fusion.119
  156.0 0.8 copy-done.15
  (77 shorter events, 4.0 us)
Async XLA Ops:
  7.2 142.7 %copy-start = (bf16[128,128]{1,0:T(8,128)(2,1)S(1)}, bf16[128,128]{1,0:T(8,128)(2,1)}, u32[]{:S(2)}) copy-start(bf16[128,128]{1,0:T(8,128)(2,1)} %param.27) | copy-start | bytes 98308
  7.2 51.0 %all-gather.2.cloned.1.call-start = ((), (), s32[]{:S(2)}) async-start(), calls=%async_computation.2 | async-start | bytes 2228224 | tf_op jit(solution)/shard_map/all_gather | solution.py:61
  11.9 2.0 %copy-start.14 = (s32[256]{0:T(256)S(1)}, s32[256]{0:T(256)}, u32[]{:S(2)}) copy-start(s32[256]{0:T(256)} %param.20) | copy-start | bytes 3076
  11.9 2.2 %copy-start.9 = (bf16[64,64]{1,0:T(8,128)(2,1)S(1)}, bf16[64,64]{1,0:T(8,128)(2,1)}, u32[]{:S(2)}) copy-start(bf16[64,64]{1,0:T(8,128)(2,1)} %param.21) | copy-start | bytes 24580
  63.8 1.3 copy-start.1
  70.4 1.0 copy-start.11
  70.4 1.1 copy-start.12
  75.0 1.0 copy-start.11
  75.0 1.1 copy-start.12
  77.0 2.3 %copy-start.6 = (bf16[128,640]{1,0:T(8,128)(2,1)S(1)}, bf16[128,640]{1,0:T(8,128)(2,1)}, u32[]{:S(2)}) copy-start(bf16[128,640]{1,0:T(8,128)(2,1)} %param.26) | copy-start | bytes 491524
  78.5 0.8 copy-start.4
  84.2 5.0 %copy-start.7 = (bf16[64,512]{1,0:T(8,128)(2,1)S(1)}, bf16[64,512]{1,0:T(8,128)(2,1)}, u32[]{:S(2)}) copy-start(bf16[64,512]{1,0:T(8,128)(2,1)} %param.24) | copy-start | bytes 196612
  84.2 5.1 %copy-start.2 = (bf16[64,128,64]{2,1,0:T(8,128)(2,1)S(1)}, bf16[64,128,64]{2,1,0:T(8,128)(2,1)}, u32[]{:S(2)}) copy-start(bf16[64,128,64]{2,1,0:T(8,128)(2,1)} %copy-done.1) | copy-start | bytes 3145732
  85.5 29.6 %all-to-all-start = ((bf16[2,32,4,16,128]{4,3,2,0,1:T(8,128)(2,1)}), bf16[2,32,4,16,128]{4,3,2,0,1:T(8,128)(2,1)}, u32[]{:S(2)}, u32[]{:S(2)}) async-start(bf16[2,32,4,16,128]{4,3,2,0,1:T(8,128)(2,1)} %copy.92), calls=%async_computation | async-start | bytes 2097152 | tf_op jit(solution)/shard_map/all_to_all | solution.py:147
  88.9 57.1 %all-reduce.2.cloned.1.call-start = ((), (), s32[]{:S(2)}) async-start(), calls=%async_computation.3 | async-start | bytes 2097152 | tf_op jit(solution)/shard_map/psum | solution.py:119
  90.6 1.5 copy-start.10
  126.7 4.7 %copy-start.8 = (bf16[256,64]{0,1:T(8,128)(2,1)S(1)}, bf16[256,64]{0,1:T(8,128)(2,1)}, u32[]{:S(2)}) copy-start(bf16[256,64]{0,1:T(8,128)(2,1)} %param.25) | copy-start | bytes 98308
  126.7 13.5 %copy-start.5 = (bf16[2048,128]{1,0:T(8,128)(2,1)S(1)}, bf16[2048,128]{1,0:T(8,128)(2,1)}, u32[]{:S(2)}) copy-start(bf16[2048,128]{1,0:T(8,128)(2,1)} %copy-done.4) | copy-start | bytes 1572868
  127.7 21.7 %all-to-all-start.1 = ((bf16[32,4,16,128]{3,2,1,0:T(8,128)(2,1)}), bf16[32,4,16,128]{3,2,1,0:T(8,128)(2,1)S(1)}, u32[]{:S(2)}, u32[]{:S(2)}) async-start(bf16[32,4,16,128]{3,2,1,0:T(8,128)(2,1)} %bitcast.34), calls=%async_computation.1 | async-start | bytes 1048576 | tf_op jit(solution)/shard_map/all_to_all | solution.py:151
  149.9 1.8 %copy-start.3 = (bf16[128,1024]{1,0:T(8,128)(2,1)S(1)}, bf16[128,1024]{1,0:T(8,128)(2,1)}, u32[]{:S(2)}) copy-start(bf16[128,1024]{1,0:T(8,128)(2,1)} %param.28) | copy-start | bytes 786436
  149.9 1.8 %copy-start.13 = (bf16[512,128]{1,0:T(8,128)(2,1)S(1)}, bf16[512,128]{1,0:T(8,128)(2,1)}, u32[]{:S(2)}) copy-start(bf16[512,128]{1,0:T(8,128)(2,1)} %param.29) | copy-start | bytes 393220
  156.0 0.8 copy-start.15
Sparse Core Ops, SparseCore 0:
  14.0 44.1 all-gather.1
  97.1 48.9 all-reduce.1
where the time goes:
time: 165 us; the launch traced here: 164 us
  waiting for transfers between devices  64.8 us (39%)
  local copies, waits for them, and re-layouts  40.2 us (24%)
  matrix products  19.4 us (12%)
  between operations  14.5 us (9%)
  blocking collectives  8.55 us (5%)
  other arithmetic  8.53 us (5%)
  starting transfers between devices  7.4 us (4%)
    all_gather x1, waiting for transfers between devices, on_device(): gathered = lax.all_gather(align_rows, 'row', axis=1, tiled=True)  42.9 us
    all_to_all x1, waiting for transfers between devices, on_device(): lax.all_to_all(grouped, ('row', 'col'), split_axis=1, concat_axis=1, tile...  18.1 us
    convert_element_type x3, local copies, waits for them, and re-layouts, triangle_product(): return product.transpose(1, 3, 0, 2, 4).astype(jnp.bfloat16)  9.76 us
    psum x1, blocking collectives, on_device(): lax.psum(partial_total.astype(jnp.bfloat16), 'col').astype(jnp.float32)  8.55 us
    unnamed x36, local copies, waits for them, and re-layouts  6.61 us
    psum x1, waiting for transfers between devices, on_device(): lax.psum(partial_sum.astype(jnp.bfloat16), 'col').astype(jnp.float32)  3.71 us
    all_to_all x1, starting transfers between devices, on_device(): lax.all_to_all(flat_result, ('row', 'col'), split_axis=0, concat_axis=0,...  3.64 us
    all_to_all x1, starting transfers between devices, on_device(): lax.all_to_all(grouped, ('row', 'col'), split_axis=1, concat_axis=1, tile...  3.46 us
  transfers between devices with their start and end apart: 4, of which 3 were waited for; matrix products, arithmetic and copies ran while one was open for 17% of the time, Pallas kernels for 0%

commit v1 on v0

--- a/solution.py
+++ b/solution.py
@@ -144,7 +144,15 @@
     factors = jnp.stack([left_side, right_side]).astype(jnp.bfloat16)
     group_size = pair_width // (n_row * n_col)
     grouped = factors.reshape(2, n_row * n_col, group_size, tok_row, tok_col)
-    received = lax.all_to_all(grouped, ("row", "col"), split_axis=1, concat_axis=1, tiled=True)
+    received = jnp.concatenate(
+        lax.all_to_all(
+            jnp.stack(jnp.split(grouped, lax.axis_size(("row", "col")), axis=1)),
+            ("row", "col"),
+            0,
+            0,
+        ),
+        axis=1,
+    )
     arranged = received.reshape(2, n_row, n_col, received.shape[2], tok_row, tok_col)
     result = triangle_product(arranged, n_row, n_col)
     flat_result = result.reshape(n_row * n_col, result.shape[2], tok_row, tok_col)

time: 165 us -> 183 us (1.11)
  other arithmetic: 8.53 us -> 27.8 us
    unnamed x1 -> x32, other arithmetic: 0.11 us -> 18.8 us
  transfers between devices with their start and end apart: 4 -> 4, of which waited for: 3 -> 3; matrix products, arithmetic and copies ran while one was open for 17% -> 15% of each run, Pallas kernels for 0% -> 0%
where the time goes in v1:
time: 183 us; the launch traced here: 182 us
  waiting for transfers between devices  64.8 us (35%)
  local copies, waits for them, and re-layouts  39 us (21%)
  other arithmetic  27.8 us (15%)
  matrix products  19.5 us (11%)
  between operations  14.5 us (8%)
  blocking collectives  8.54 us (5%)
  starting transfers between devices  7.39 us (4%)
    all_gather x1, waiting for transfers between devices, on_device(): gathered = lax.all_gather(align_rows, 'row', axis=1, tiled=True)  42.9 us
    unnamed x32, other arithmetic  18.8 us
    all_to_all x1, waiting for transfers between devices, on_device(): lax.all_to_all(jnp.stack(jnp.split(grouped, lax.axis_size(('row', 'col'))...  18.1 us
    convert_element_type x3, local copies, waits for them, and re-layouts, triangle_product(): return product.transpose(1, 3, 0, 2, 4).astype(jnp.bfloat16)  9.76 us
    psum x1, blocking collectives, on_device(): lax.psum(partial_total.astype(jnp.bfloat16), 'col').astype(jnp.float32)  8.54 us
    unnamed x36, local copies, waits for them, and re-layouts  6.6 us
    psum x1, waiting for transfers between devices, on_device(): lax.psum(partial_sum.astype(jnp.bfloat16), 'col').astype(jnp.float32)  3.71 us
  transfers between devices with their start and end apart: 4, of which 3 were waited for; matrix products, arithmetic and copies ran while one was open for 15% of the time, Pallas kernels for 0%

profile of v1, /device:TPU:0, one launch (start us, length us, event | category | flops | bytes accessed | tf_op | source)
XLA Modules:
  0.0 181.6 jit_solution(9011661152855975141)
XLA Ops:
  7.2 0.7 compare_select_fusion
  7.9 0.7 compare_and_fusion
  8.5 2.0 %copy.172 = bf16[256,16,64]{2,1,0:T(8,128)(2,1)S(1)} copy(bf16[256,16,64]{0,2,1:T(8,128)(2,1)} %param.18) | data formatting | bytes 1048576 | tf_op args[1]
  10.6 0.6 gather_fusion
  13.1 0.8 divide_convert_fusion
  14.1 1.2 convolution_convert_fusion.2
  15.3 42.9 %all-gather.2.cloned.1.call-done = bf16[64,16384]{1,0:T(8,128)(2,1)} async-done(((bf16[64,1024]{1,0:T(8,128)(2,1)}), bf16[64,16384]{1,0:T(8,128)(2,1)}) %all-gather.2.cloned.1.call-update) | async-done | bytes 2097168 | tf_op jit(solution)/shard_map/all_gather | solution.py:61
  58.2 2.3 %constant_dynamic-slice_fusion.1 = bf16[64,8192]{1,0:T(8,128)(2,1)} fusion(bf16[64,16384]{1,0:T(8,128)(2,1)} %all-gather.2.cloned.1.call-done, s32[]{:T(128)S(6)} %select_n.24), kind=kLoop, calls=%fused_computation.242 | loop fusion | bytes 2097156 | tf_op jit(solution)/shard_map/dynamic_slice | solution.py:62
  60.5 3.3 %reshape.296 = bf16[64,128,64]{2,1,0:T(8,128)(2,1)S(1)} reshape(bf16[64,8192]{1,0:T(8,128)(2,1)} %constant_dynamic-slice_fusion.1) | data formatting | bytes 2097152 | tf_op jit(solution)/shard_map/reshape | solution.py:65
  63.8 1.3 copy-done.1
  65.1 0.9 convolution_convert_fusion.1
  66.0 1.7 copy.179
  67.7 9.3 %while.20 = (s32[]{:T(128)}, bf16[2,8,128,128]{3,2,1,0:T(8,128)(2,1)S(1)}, bf16[2,8,128,128]{3,2,1,0:T(8,128)(2,1)}, bf16[2,64,256]{1,2,0:T(8,128)(2,1)}, bf16[6...) while((s32[]{:T(128)}, bf16[2,8,128,128]{3,2,1,0:T(8,128)(2,1)S(1)}, ...), condition=%wide.region_3.4_spmd, body=%wide.region_2.3_spmd.sunk | while | flops 405143552 | bytes 13992077 | solution.py:98
  67.7 0.8 constant_dynamic-slice_fusion.3
  68.6 1.1 copy.297
  69.7 0.7 fusion.143
  70.4 0.8 copy.298
  71.5 0.9 fusion.144
  72.4 0.8 constant_dynamic-slice_fusion.3
  73.2 1.1 copy.297
  74.3 0.7 fusion.143
  75.0 0.8 copy.298
  76.1 0.9 fusion.144
  77.2 0.6 fusion.47
  77.9 0.6 fusion.45
  78.5 0.8 copy-done.4
  79.3 0.7 convolution_bitcast_fusion
  80.0 1.6 slice_multiply_fusion.2
  82.1 1.6 copy.181
  87.1 0.6 constant_dynamic-update-slice_fusion.26
  88.3 0.6 constant_dynamic-update-slice_fusion.24
  89.6 0.6 constant_dynamic-update-slice_fusion.22
  93.2 0.6 constant_dynamic-update-slice_fusion.16
  95.6 0.6 constant_dynamic-update-slice_fusion.12
  96.8 0.6 constant_dynamic-update-slice_fusion.10
  99.2 0.6 constant_dynamic-update-slice_fusion.6
  100.4 0.6 constant_dynamic-update-slice_fusion.4
  102.9 0.6 constant_dynamic-update-slice_fusion
  103.5 3.4 %all-to-all-start = ((bf16[32,2,1,4,16,128]{5,4,3,1,2,0:T(8,128)(2,1)}), bf16[32,2,1,4,16,128]{5,4,3,1,2,0:T(8,128)(2,1)}, u32[]{:S(2)}, u32[]{:S(2)}) async-start(bf16[32,2,1,4,16,128]{5,4,3,1,2,0:T(8,128)(2,1)} %constant_dynamic-update-slice_fusion), calls=%async_computation | async-start | bytes 2097152 | tf_op jit(solution)/shard_map/all_to_all | solution.py:148
  107.3 1.3 convert_bitcast_fusion.1
  108.6 0.9 copy.219
  109.5 0.6 fusion.43
  110.5 1.2 convolution_convert_fusion
  111.7 1.6 reshape.305
  113.3 1.6 copy.222
  115.0 18.1 %all-to-all-done = bf16[32,2,1,4,16,128]{5,4,3,1,2,0:T(8,128)(2,1)} async-done(((bf16[32,2,1,4,16,128]{5,4,3,1,2,0:T(8,128)(2,1)}), bf16[32,2,1,4,16,128]{5,4,3,1,2,0:T(8,128)(2,1)}, u32[]{:S(2)}, u32[]{:S(2)}) %all-to-all-start) | async-done | bytes 1048608 | tf_op jit(solution)/shard_map/all_to_all | solution.py:148
  133.1 1.4 fusion.108
  134.6 1.3 bitcast_convert_fusion
  135.9 3.0 %copy.214 = bf16[4,16,16,16,16]{4,3,2,1,0:T(8,128)(2,1)} copy(bf16[4,16,16,16,16]{4,2,3,1,0:T(8,128)(2,1)S(1)} %bitcast_convert_fusion) | data formatting | bytes 1048576 | tf_op jit(solution)/shard_map/convert_element_type | solution.py:26
  138.9 5.8 %convert_element_type.146 = bf16[4,16,16,2,128]{4,3,2,1,0:T(2,128)(2,1)S(1)} reshape(bf16[4,16,16,16,16]{4,3,2,1,0:T(8,128)(2,1)} %copy.214) | data formatting | bytes 1048576 | tf_op jit(solution)/shard_map/convert_element_type | solution.py:26
  144.7 0.9 copy.215
  145.6 3.6 %all-to-all-start.1 = ((bf16[32,4,16,128]{3,2,1,0:T(8,128)(2,1)}), bf16[32,4,16,128]{3,2,1,0:T(8,128)(2,1)S(1)}, u32[]{:S(2)}, u32[]{:S(2)}) async-start(bf16[32,4,16,128]{3,2,1,0:T(8,128)(2,1)} %bitcast.67), calls=%async_computation.1 | async-start | bytes 1048576 | tf_op jit(solution)/shard_map/all_to_all | solution.py:159
  149.6 8.5 %psum.15 = bf16[8,16]{1,0:T(8,128)(2,1)S(1)} all-reduce(bf16[8,16]{1,0:T(8,128)(2,1)S(1)} %copy.223), channel_id=1, replica_groups=mesh['groups'=1,'row'=16,'col'=2] {'col'}, use_global_device_ids=true, to_apply=%region_14.15 | all-reduce | flops 128 | bytes 512 | tf_op jit(solution)/shard_map/psum | solution.py:120
  158.2 2.2 %fusion.26 = f32[2048,128]{1,0:T(8,128)} fusion(bf16[2048,128]{1,0:T(8,128)(2,1)S(1)} %copy-done.5, bf16[128,640]{1,0:T(8,128)(2,1)} %param.26), kind=kOutput, calls=%fused_computation.101 | convolution fusion | flops 67895296 | bytes 1605632 | tf_op jit(solution)/shard_map/dot_general | solution.py:166
  160.3 3.7 %all-reduce.2.cloned.1.call-done = bf16[8,16,64,32]{2,3,1,0:T(8,128)(2,1)} async-done(((bf16[8,16,64,32]{2,3,1,0:T(8,128)(2,1)}), bf16[8,16,64,32]{2,3,1,0:T(8,128)(2,1)}) %all-reduce.2.cloned.1.call-update) | async-done | bytes 524304 | tf_op jit(solution)/shard_map/psum | solution.py:119
  164.0 2.5 %fusion.32 = bf16[64,16,64]{2,0,1:T(8,128)(2,1)S(1)} fusion(bf16[8,32,64,1]{2,1,3,0:T(8,128)(2,1)S(1)} %bitcast.366, bf16[8,16,64,32]{2,3,1,0:T(8,128)(2,1)} %all-reduce.2.cloned.1.call-done, bf16[64,8,32,1]{0,2,3,1:T(8,128)(2,1)S(1)} %bitcast.365, f32[8,16]{1,0:T(8,128)S(1)} %convert_element_type.161, f32[64,16]{0,1:T(8,128)S(1)} %add_sqrt_fusion.2, ...), kind=kOutput, calls=%fused_computation.111 | convolution fusion | flops 69533696 | bytes 860736 | tf_op jit(solution)/shard_map/hisc,hcm->sim/dot_general | solution.py:127
  166.5 0.9 copy.225
  167.9 1.8 fusion.27
  169.8 4.2 %while.21 = (s32[]{:T(128)}, bf16[2,1024,128]{2,1,0:T(8,128)(2,1)S(1)}, bf16[2,1024,128]{2,1,0:T(8,128)(2,1)S(1)}, bf16[128,1024]{1,0:T(8,128)(2,1)S(1)}, bf16[512,128]{1,0:T(8,128)(2,1)S(1)}, /*index=5*/s32[]{:T(128)}) while((s32[]{:T(128)}, bf16[2,1024,128]{2,1,0:T(8,128)(2,1)S(1)}, bf16[2,1024,128]{2,1,0:T(8,128)(2,1)S(1)}, ...), condition=%wide.region_11.12_spmd, body=%wide.region_8.11_spmd.sunk | while | flops 407503872 | bytes 10129493 | solution.py:184
  170.3 0.8 fusion.150
  171.1 0.8 fusion.151
  172.4 0.8 fusion.150
  173.2 0.8 fusion.151
  174.0 0.8 copy-done.15
  (107 shorter events, 20.4 us)
Async XLA Ops:
  7.2 160.7 %copy-start = (bf16[128,128]{1,0:T(8,128)(2,1)S(1)}, bf16[128,128]{1,0:T(8,128)(2,1)}, u32[]{:S(2)}) copy-start(bf16[128,128]{1,0:T(8,128)(2,1)} %param.27) | copy-start | bytes 98308
  7.2 51.0 %all-gather.2.cloned.1.call-start = ((), (), s32[]{:S(2)}) async-start(), calls=%async_computation.2 | async-start | bytes 2228224 | tf_op jit(solution)/shard_map/all_gather | solution.py:61
  11.9 2.0 %copy-start.14 = (s32[256]{0:T(256)S(1)}, s32[256]{0:T(256)}, u32[]{:S(2)}) copy-start(s32[256]{0:T(256)} %param.20) | copy-start | bytes 3076
  11.9 2.2 %copy-start.9 = (bf16[64,64]{1,0:T(8,128)(2,1)S(1)}, bf16[64,64]{1,0:T(8,128)(2,1)}, u32[]{:S(2)}) copy-start(bf16[64,64]{1,0:T(8,128)(2,1)} %param.21) | copy-start | bytes 24580
  63.8 1.3 copy-start.1
  70.4 1.0 copy-start.11
  70.4 1.1 copy-start.12
  75.0 1.0 copy-start.11
  75.0 1.1 copy-start.12
  77.0 2.3 %copy-start.6 = (bf16[128,640]{1,0:T(8,128)(2,1)S(1)}, bf16[128,640]{1,0:T(8,128)(2,1)}, u32[]{:S(2)}) copy-start(bf16[128,640]{1,0:T(8,128)(2,1)} %param.26) | copy-start | bytes 491524
  78.5 0.8 copy-start.4
  102.2 5.0 %copy-start.7 = (bf16[64,512]{1,0:T(8,128)(2,1)S(1)}, bf16[64,512]{1,0:T(8,128)(2,1)}, u32[]{:S(2)}) copy-start(bf16[64,512]{1,0:T(8,128)(2,1)} %param.24) | copy-start | bytes 196612
  102.2 5.1 %copy-start.2 = (bf16[64,128,64]{2,1,0:T(8,128)(2,1)S(1)}, bf16[64,128,64]{2,1,0:T(8,128)(2,1)}, u32[]{:S(2)}) copy-start(bf16[64,128,64]{2,1,0:T(8,128)(2,1)} %copy-done.1) | copy-start | bytes 3145732
  103.5 29.6 %all-to-all-start = ((bf16[32,2,1,4,16,128]{5,4,3,1,2,0:T(8,128)(2,1)}), bf16[32,2,1,4,16,128]{5,4,3,1,2,0:T(8,128)(2,1)}, u32[]{:S(2)}, u32[]{:S(2)}) async-start(bf16[32,2,1,4,16,128]{5,4,3,1,2,0:T(8,128)(2,1)} %constant_dynamic-update-slice_fusion), calls=%async_computation | async-start | bytes 2097152 | tf_op jit(solution)/shard_map/all_to_all | solution.py:148
  106.9 57.1 %all-reduce.2.cloned.1.call-start = ((), (), s32[]{:S(2)}) async-start(), calls=%async_computation.3 | async-start | bytes 2097152 | tf_op jit(solution)/shard_map/psum | solution.py:119
  108.6 1.5 copy-start.10
  144.7 4.7 %copy-start.8 = (bf16[256,64]{0,1:T(8,128)(2,1)S(1)}, bf16[256,64]{0,1:T(8,128)(2,1)}, u32[]{:S(2)}) copy-start(bf16[256,64]{0,1:T(8,128)(2,1)} %param.25) | copy-start | bytes 98308
  144.7 13.5 %copy-start.5 = (bf16[2048,128]{1,0:T(8,128)(2,1)S(1)}, bf16[2048,128]{1,0:T(8,128)(2,1)}, u32[]{:S(2)}) copy-start(bf16[2048,128]{1,0:T(8,128)(2,1)} %copy-done.4) | copy-start | bytes 1572868
  145.6 21.8 %all-to-all-start.1 = ((bf16[32,4,16,128]{3,2,1,0:T(8,128)(2,1)}), bf16[32,4,16,128]{3,2,1,0:T(8,128)(2,1)S(1)}, u32[]{:S(2)}, u32[]{:S(2)}) async-start(bf16[32,4,16,128]{3,2,1,0:T(8,128)(2,1)} %bitcast.67), calls=%async_computation.1 | async-start | bytes 1048576 | tf_op jit(solution)/shard_map/all_to_all | solution.py:159
  167.9 1.8 %copy-start.3 = (bf16[128,1024]{1,0:T(8,128)(2,1)S(1)}, bf16[128,1024]{1,0:T(8,128)(2,1)}, u32[]{:S(2)}) copy-start(bf16[128,1024]{1,0:T(8,128)(2,1)} %param.28) | copy-start | bytes 786436
  167.9 1.8 %copy-start.13 = (bf16[512,128]{1,0:T(8,128)(2,1)S(1)}, bf16[512,128]{1,0:T(8,128)(2,1)}, u32[]{:S(2)}) copy-start(bf16[512,128]{1,0:T(8,128)(2,1)} %param.29) | copy-start | bytes 393220
  174.0 0.8 copy-start.15
Sparse Core Ops, SparseCore 0:
  14.0 44.1 all-gather.1
  115.1 48.9 all-reduce.1
